TPU v7x, 128 devices: a whole 4x4x4 slice. The times are simulated.
128 devices in a mesh: row: 16 (over y, z), col: 8 (over x, core).
Axes of the slice: x: 4, y: 4, z: 4, core: 2. Of those that a mesh axis runs over, the one named last changes fastest.
Arguments:
- fock_matrix: bfloat16 [3072, 3072], P('row', 'col'), as said below
- density: bfloat16 [3072, 3072], P('row', 'col'), as said below
- margin: bfloat16 [3072, 3072], P('row', 'col'), as said below
- fill_patterns: int32 [3, 96, 96], P(None, 'row', 'col'), may hold values from 0 to 1, as said below
- first_filters: int32 [3, 96, 96], P(None, 'row', 'col'), may hold values from 0 to 1, as said below
- owner_order: int32 [96], replicated, may hold values from 0 to 95, as said below
- second_filters: int32 [7, 96, 96], P(None, 'row', 'col'), may hold values from 0 to 1, as said below
Outputs:
- evolved: bfloat16 [3072, 3072], P('row', 'col')
Inputs may be any that keep to these rules, and one draw needn't show every extreme that they name: `fock_matrix`: Symmetric. `density`: Symmetric. `margin`: Symmetric, with unit diagonal. `fill_patterns`: each entry says whether a block is kept; each pattern is symmetric and keeps every diagonal block. `first_filters`: each entry says whether a block of the product is kept; each filter is symmetric and keeps every diagonal block. `second_filters`: each entry says whether a block of the product is kept, indexed in owner order; each filter is symmetric and keeps every diagonal block. `owner_order`: A permutation of the 96 block indices.
All inputs are finite; a program needn't handle non-finite values.
Results may differ from a plain program's by a relative error of at most 0.012.
Values may be sent and summed in bfloat16 or wider, within the bound.
A program may use at most 64 MiB of HBM per device.

v0:
```python
import jax
import jax.numpy as jnp
from jax import lax
from jax.sharding import PartitionSpec as P

BLK = 32
TERMS = 6
SQUARINGS = 2


def expand(mask, values):
    row_blocks = mask.shape[0]
    column_blocks = mask.shape[1]
    shaped = values.reshape(row_blocks, BLK, column_blocks, BLK) * mask[:, None, :, None].astype(
        values.dtype
    )
    return shaped.reshape(values.shape)


def panel_rows(matrix):
    return lax.all_gather(matrix, "col", axis=1, tiled=True)


def panel_times(row_panel, matrix):
    return jnp.dot(
        row_panel,
        lax.all_gather(matrix, "row", axis=0, tiled=True),
        preferred_element_type=jnp.float32,
    )


def reorder(generator, owner_order):
    row_blocks = generator.shape[0] // BLK
    column_blocks = generator.shape[1] // BLK
    wanted_rows = lax.dynamic_slice_in_dim(
        owner_order, lax.axis_index("row") * row_blocks, row_blocks
    )
    wanted_columns = lax.dynamic_slice_in_dim(
        owner_order, lax.axis_index("col") * column_blocks, column_blocks
    )
    segment = lax.all_gather(generator, "row", axis=0, tiled=True)
    arriving = segment.shape[0] // BLK
    source = jnp.arange(arriving, dtype=jnp.int32)
    select = (wanted_rows[:, None] == source[None, :]).astype(jnp.bfloat16)
    flattened = segment.reshape(arriving, -1)
    by_rows = jnp.dot(select, flattened, preferred_element_type=jnp.float32)
    by_rows = by_rows.reshape(generator.shape).astype(jnp.bfloat16)
    segment = lax.all_gather(by_rows, "col", axis=1, tiled=True)
    arriving = segment.shape[1] // BLK
    source = jnp.arange(arriving, dtype=jnp.int32)
    select = (source[:, None] == wanted_columns[None, :]).astype(jnp.bfloat16)
    shaped = segment.reshape(segment.shape[0], arriving, BLK)
    placed = jnp.einsum("pjk,ji->pik", shaped, select, preferred_element_type=jnp.float32)
    return placed.reshape(generator.shape).astype(jnp.bfloat16)


def on_device(
    fock_matrix, density, margin, fill_patterns, first_filters, owner_order, second_filters
):
    masked_fock = expand(fill_patterns[0], fock_matrix)
    masked_density = expand(fill_patterns[1], density)
    masked_margin = expand(fill_patterns[2], margin)
    fock_density = expand(
        first_filters[0], panel_times(panel_rows(masked_fock), masked_density)
    ).astype(jnp.bfloat16)
    margin_density = expand(
        first_filters[1], panel_times(panel_rows(masked_margin), masked_density)
    ).astype(jnp.bfloat16)
    generator = panel_times(panel_rows(fock_density), masked_margin) - panel_times(
        panel_rows(margin_density), masked_fock
    )
    generator = expand(first_filters[2], generator).astype(jnp.bfloat16)
    reordered = reorder(generator, owner_order)
    scaled = (reordered.astype(jnp.float32) * 0.25).astype(jnp.bfloat16)
    rows_here, columns_here = scaled.shape
    row_ids = lax.axis_index("row") * rows_here + jnp.arange(rows_here, dtype=jnp.int32)
    column_ids = lax.axis_index("col") * columns_here + jnp.arange(columns_here, dtype=jnp.int32)
    identity = (row_ids[:, None] == column_ids[None, :]).astype(jnp.float32)
    scaled_rows = panel_rows(scaled)
    series = (identity + scaled.astype(jnp.float32) / 6.0).astype(jnp.bfloat16)
    for number in range(TERMS - 1):
        degree = TERMS - 1 - number
        series = (
            identity + expand(second_filters[number], panel_times(scaled_rows, series)) / degree
        ).astype(jnp.bfloat16)
    for number in range(SQUARINGS):
        series = expand(
            second_filters[TERMS - 1 + number], panel_times(panel_rows(series), series)
        ).astype(jnp.bfloat16)
    return series


def solution(mesh):
    return jax.shard_map(
        on_device,
        mesh=mesh,
        in_specs=(
            P("row", "col"),
            P("row", "col"),
            P("row", "col"),
            P(None, "row", "col"),
            P(None, "row", "col"),
            P(),
            P(None, "row", "col"),
        ),
        out_specs=P("row", "col"),
        check_vma=False,
    )
```

profile of v0, /device:TPU:0, one launch (start us, length us, event | category | flops | bytes accessed | tf_op | source)
XLA Modules:
  0.0 756.5 jit_solution(15816942738153316803)
XLA Ops:
  12.9 22.2 %all-gather.20.cloned.1.call-done = bf16[192,3072]{1,0:T(8,128)(2,1)} async-done(((bf16[192,384]{1,0:T(8,128)(2,1)}), bf16[192,3072]{1,0:T(8,128)(2,1)}) %all-gather.20.cloned.1.call-update) | async-done | bytes 1179664 | tf_op jit(solution)/shard_map/all_gather | solution.py:21
  35.1 47.9 %all-gather.22.cloned.1.call-done = bf16[3072,384]{1,0:T(8,128)(2,1)} async-done(((bf16[192,384]{1,0:T(8,128)(2,1)}), bf16[3072,384]{1,0:T(8,128)(2,1)}) %all-gather.22.cloned.1.call-update) | async-done | bytes 2359312 | tf_op jit(solution)/shard_map/all_gather | solution.py:27
  82.9 3.5 fusion.32
  90.3 17.1 %all-gather.28.cloned.1.call-done = bf16[192,3072]{1,0:T(8,128)(2,1)} async-done(((bf16[192,384]{1,0:T(8,128)(2,1)}), bf16[192,3072]{1,0:T(8,128)(2,1)}) %all-gather.28.cloned.1.call-update) | async-done | bytes 1179664 | tf_op jit(solution)/shard_map/all_gather | solution.py:21
  110.8 44.3 %all-gather.26.cloned.1.call-done = bf16[3072,384]{1,0:T(8,128)(2,1)} async-done(((bf16[192,384]{1,0:T(8,128)(2,1)}), bf16[3072,384]{1,0:T(8,128)(2,1)}) %all-gather.26.cloned.1.call-update) | async-done | bytes 2359312 | tf_op jit(solution)/shard_map/all_gather | solution.py:27
  155.1 24.3 %all-gather.24.cloned.1.call-done = bf16[192,3072]{1,0:T(8,128)(2,1)} async-done(((bf16[192,384]{1,0:T(8,128)(2,1)}), bf16[192,3072]{1,0:T(8,128)(2,1)}) %all-gather.24.cloned.1.call-update) | async-done | bytes 1179664 | tf_op jit(solution)/shard_map/all_gather | solution.py:21
  182.3 44.9 %all-gather.32.cloned.1.call-done = bf16[3072,384]{1,0:T(8,128)(2,1)} async-done(((bf16[192,384]{1,0:T(8,128)(2,1)}), bf16[3072,384]{1,0:T(8,128)(2,1)}) %all-gather.32.cloned.1.call-update) | async-done | bytes 2359312 | tf_op jit(solution)/shard_map/all_gather | solution.py:27
  227.2 24.5 %all-gather.30.cloned.1.call-done = bf16[192,3072]{1,0:T(8,128)(2,1)} async-done(((bf16[192,384]{1,0:T(8,128)(2,1)}), bf16[192,3072]{1,0:T(8,128)(2,1)}) %all-gather.30.cloned.1.call-update) | async-done | bytes 1179664 | tf_op jit(solution)/shard_map/all_gather | solution.py:21
  251.7 3.5 fusion.34
  255.3 45.7 %all-gather.34.cloned.1.call-done = bf16[3072,384]{1,0:T(8,128)(2,1)} async-done(((bf16[192,384]{1,0:T(8,128)(2,1)}), bf16[3072,384]{1,0:T(8,128)(2,1)}) %all-gather.34.cloned.1.call-update) | async-done | bytes 2359312 | tf_op jit(solution)/shard_map/all_gather | solution.py:41
  305.7 23.5 %all-gather.36.cloned.1.call-done = bf16[192,3072]{0,1:T(8,128)(2,1)} async-done(((bf16[192,384]{0,1:T(8,128)(2,1)}), bf16[192,3072]{0,1:T(8,128)(2,1)}) %all-gather.36.cloned.1.call-update) | async-done | bytes 1179664 | tf_op jit(solution)/shard_map/all_gather | solution.py:48
  335.0 22.0 %all-gather.38.cloned.1.call-done = bf16[192,3072]{0,1:T(8,128)(2,1)} async-done(((bf16[192,384]{0,1:T(8,128)(2,1)}), bf16[192,3072]{0,1:T(8,128)(2,1)}) %all-gather.38.cloned.1.call-update) | async-done | bytes 1179664 | tf_op jit(solution)/shard_map/all_gather | solution.py:21
  357.0 48.1 %all-gather.40.cloned.1.call-done = bf16[3072,384]{1,0:T(8,128)(2,1)} async-done(((bf16[192,384]{1,0:T(8,128)(2,1)}), bf16[3072,384]{1,0:T(8,128)(2,1)}) %all-gather.40.cloned.1.call-update) | async-done | bytes 2359312 | tf_op jit(solution)/shard_map/all_gather | solution.py:27
  405.1 3.6 fusion.31
  409.6 44.2 %all-gather.42.cloned.1.call-done = bf16[3072,384]{1,0:T(8,128)(2,1)} async-done(((bf16[192,384]{1,0:T(8,128)(2,1)}), bf16[3072,384]{1,0:T(8,128)(2,1)}) %all-gather.42.cloned.1.call-update) | async-done | bytes 2359312 | tf_op jit(solution)/shard_map/all_gather | solution.py:27
  457.7 44.4 %all-gather.44.cloned.1.call-done = bf16[3072,384]{1,0:T(8,128)(2,1)} async-done(((bf16[192,384]{1,0:T(8,128)(2,1)}), bf16[3072,384]{1,0:T(8,128)(2,1)}) %all-gather.44.cloned.1.call-update) | async-done | bytes 2359312 | tf_op jit(solution)/shard_map/all_gather | solution.py:27
  505.9 44.4 %all-gather.46.cloned.1.call-done = bf16[3072,384]{1,0:T(8,128)(2,1)} async-done(((bf16[192,384]{1,0:T(8,128)(2,1)}), bf16[3072,384]{1,0:T(8,128)(2,1)}) %all-gather.46.cloned.1.call-update) | async-done | bytes 2359312 | tf_op jit(solution)/shard_map/all_gather | solution.py:27
  554.1 44.4 %all-gather.48.cloned.1.call-done = bf16[3072,384]{1,0:T(8,128)(2,1)} async-done(((bf16[192,384]{1,0:T(8,128)(2,1)}), bf16[3072,384]{1,0:T(8,128)(2,1)}) %all-gather.48.cloned.1.call-update) | async-done | bytes 2359312 | tf_op jit(solution)/shard_map/all_gather | solution.py:27
  603.0 21.6 %all-gather.50.cloned.1.call-done = bf16[192,3072]{1,0:T(8,128)(2,1)} async-done(((bf16[192,384]{1,0:T(8,128)(2,1)}), bf16[192,3072]{1,0:T(8,128)(2,1)}) %all-gather.50.cloned.1.call-update) | async-done | bytes 1179664 | tf_op jit(solution)/shard_map/all_gather | solution.py:21
  624.6 47.7 %all-gather.52.cloned.1.call-done = bf16[3072,384]{1,0:T(8,128)(2,1)} async-done(((bf16[192,384]{1,0:T(8,128)(2,1)}), bf16[3072,384]{1,0:T(8,128)(2,1)}) %all-gather.52.cloned.1.call-update) | async-done | bytes 2359312 | tf_op jit(solution)/shard_map/all_gather | solution.py:27
  672.3 3.5 fusion.35
  677.2 21.5 %all-gather.54.cloned.1.call-done = bf16[192,3072]{1,0:T(8,128)(2,1)} async-done(((bf16[192,384]{1,0:T(8,128)(2,1)}), bf16[192,3072]{1,0:T(8,128)(2,1)}) %all-gather.54.cloned.1.call-update) | async-done | bytes 1179664 | tf_op jit(solution)/shard_map/all_gather | solution.py:21
  698.7 47.9 %all-gather.56.cloned.1.call-done = bf16[3072,384]{1,0:T(8,128)(2,1)} async-done(((bf16[192,384]{1,0:T(8,128)(2,1)}), bf16[3072,384]{1,0:T(8,128)(2,1)}) %all-gather.56.cloned.1.call-update) | async-done | bytes 2359312 | tf_op jit(solution)/shard_map/all_gather | solution.py:27
  746.5 3.5 fusion.36
  (109 shorter events, 44.9 us)
Async XLA Ops:
  6.5 28.5 %all-gather.20.cloned.1.call-start = ((), (), s32[]{:S(2)}) async-start(), calls=%async_computation | async-start | bytes 1327104 | tf_op jit(solution)/shard_map/all_gather | solution.py:21
  8.7 74.2 %all-gather.22.cloned.1.call-start = ((), (), s32[]{:S(2)}) async-start(), calls=%async_computation.1 | async-start | bytes 2506752 | tf_op jit(solution)/shard_map/all_gather | solution.py:27
  9.4 2.8 copy-start.5
  10.2 97.2 %all-gather.28.cloned.1.call-start = ((), (), s32[]{:S(2)}) async-start(), calls=%async_computation.4 | async-start | bytes 1327104 | tf_op jit(solution)/shard_map/all_gather | solution.py:21
  11.6 143.6 %all-gather.26.cloned.1.call-start = ((), (), s32[]{:S(2)}) async-start(), calls=%async_computation.3 | async-start | bytes 2506752 | tf_op jit(solution)/shard_map/all_gather | solution.py:27
  12.2 167.3 %all-gather.24.cloned.1.call-start = ((), (), s32[]{:S(2)}) async-start(), calls=%async_computation.2 | async-start | bytes 1327104 | tf_op jit(solution)/shard_map/all_gather | solution.py:21
  86.4 140.8 %all-gather.32.cloned.1.call-start = ((), (), s32[]{:S(2)}) async-start(), calls=%async_computation.6 | async-start | bytes 2506752 | tf_op jit(solution)/shard_map/all_gather | solution.py:27
  87.0 164.7 %all-gather.30.cloned.1.call-start = ((), (), s32[]{:S(2)}) async-start(), calls=%async_computation.5 | async-start | bytes 1327104 | tf_op jit(solution)/shard_map/all_gather | solution.py:21
  87.0 20.4 %copy-start = (bf16[3072,384]{1,0:T(8,128)(2,1)S(1)}, bf16[3072,384]{1,0:T(8,128)(2,1)}, u32[]{:S(2)}) copy-start(bf16[3072,384]{1,0:T(8,128)(2,1)} %all-gather.22.cloned.1.call-done) | copy-start | bytes 7077892
  110.1 190.8 %all-gather.34.cloned.1.call-start = ((), (), s32[]{:S(2)}) async-start(), calls=%async_computation.7 | async-start | bytes 2506752 | tf_op jit(solution)/shard_map/all_gather | solution.py:41
  182.3 73.0 %copy-start.7 = (s32[96]{0:T(128)S(1)}, s32[96]{0:T(128)}, u32[]{:S(2)}) copy-start(s32[96]{0:T(128)} %param.12) | copy-start | bytes 1156
  255.2 74.1 %all-gather.36.cloned.1.call-start = ((), (), s32[]{:S(2)}) async-start(), calls=%async_computation.8 | async-start | bytes 1769472 | tf_op jit(solution)/shard_map/all_gather | solution.py:48
  305.6 51.4 %all-gather.38.cloned.1.call-start = ((), (), s32[]{:S(2)}) async-start(), calls=%async_computation.9 | async-start | bytes 1769472 | tf_op jit(solution)/shard_map/all_gather | solution.py:21
  329.2 5.1 copy-start.4
  332.3 72.8 %all-gather.40.cloned.1.call-start = ((), (), s32[]{:S(2)}) async-start(), calls=%async_computation.10 | async-start | bytes 2506752 | tf_op jit(solution)/shard_map/all_gather | solution.py:27
  334.3 119.5 %all-gather.42.cloned.1.call-start = ((), (), s32[]{:S(2)}) async-start(), calls=%async_computation.11 | async-start | bytes 2506752 | tf_op jit(solution)/shard_map/all_gather | solution.py:27
  408.7 93.3 %all-gather.44.cloned.1.call-start = ((), (), s32[]{:S(2)}) async-start(), calls=%async_computation.12 | async-start | bytes 2506752 | tf_op jit(solution)/shard_map/all_gather | solution.py:27
  409.0 44.8 %copy-start.6 = (bf16[192,3072]{0,1:T(8,128)(2,1)S(1)}, bf16[192,3072]{0,1:T(8,128)(2,1)}, u32[]{:S(2)}) copy-start(bf16[192,3072]{0,1:T(8,128)(2,1)} %all-gather.38.cloned.1.call-done) | copy-start | bytes 3538948
  457.0 93.3 %all-gather.46.cloned.1.call-start = ((), (), s32[]{:S(2)}) async-start(), calls=%async_computation.13 | async-start | bytes 2506752 | tf_op jit(solution)/shard_map/all_gather | solution.py:27
  505.2 93.3 %all-gather.48.cloned.1.call-start = ((), (), s32[]{:S(2)}) async-start(), calls=%async_computation.14 | async-start | bytes 2506752 | tf_op jit(solution)/shard_map/all_gather | solution.py:27
  553.4 71.1 %all-gather.50.cloned.1.call-start = ((), (), s32[]{:S(2)}) async-start(), calls=%async_computation.15 | async-start | bytes 1327104 | tf_op jit(solution)/shard_map/all_gather | solution.py:21
  601.7 70.6 %all-gather.52.cloned.1.call-start = ((), (), s32[]{:S(2)}) async-start(), calls=%async_computation.16 | async-start | bytes 2506752 | tf_op jit(solution)/shard_map/all_gather | solution.py:27
  602.3 96.4 %all-gather.54.cloned.1.call-start = ((), (), s32[]{:S(2)}) async-start(), calls=%async_computation.17 | async-start | bytes 1327104 | tf_op jit(solution)/shard_map/all_gather | solution.py:21
  675.8 70.8 %all-gather.56.cloned.1.call-start = ((), (), s32[]{:S(2)}) async-start(), calls=%async_computation.18 | async-start | bytes 2506752 | tf_op jit(solution)/shard_map/all_gather | solution.py:27
  (3 other events, 5.3 us)
Sparse Core Ops, SparseCore 0:
  9.0 25.9 all-gather.19
  37.2 45.6 all-gather.21
  84.6 22.7 all-gather.27
  109.4 45.6 all-gather.25
  156.7 22.7 all-gather.23
  181.5 45.6 all-gather.31
  228.9 22.7 all-gather.29
  255.3 45.6 all-gather.33
  305.7 23.4 all-gather.35
  332.5 24.4 all-gather.37
  359.2 45.8 all-gather.39
  408.9 44.8 all-gather.41
  457.1 44.8 all-gather.43
  505.3 44.8 all-gather.45
  553.6 44.8 all-gather.47
  601.8 22.7 all-gather.49
  626.6 45.6 all-gather.51
  675.9 22.7 all-gather.53
  700.8 45.6 all-gather.55
where the time goes:
time: 757 us
  waiting for transfers between devices  683 us (90%)
  matrix products  38.5 us (5%)
  local copies, waits for them, and re-layouts  16.9 us (2%)
  between operations  13.7 us (2%)
    all_gather x10, waiting for transfers between devices, panel_times(): lax.all_gather(matrix, 'row', axis=0, tiled=True)  458 us
    all_gather x7, waiting for transfers between devices, panel_rows(): return lax.all_gather(matrix, 'col', axis=1, tiled=True)  153 us
    all_gather x1, waiting for transfers between devices, reorder(): segment = lax.all_gather(generator, 'row', axis=0, tiled=True)  45.7 us
    dot_general x11, matrix products, panel_times(): jnp.dot(row_panel, lax.all_gather(matrix, 'row', axis=0, tiled=True), pre...  35.6 us
    all_gather x1, waiting for transfers between devices, reorder(): segment = lax.all_gather(by_rows, 'col', axis=1, tiled=True)  23.5 us
  transfers between devices with their start and end apart: 19, of which 19 were waited for; matrix products, arithmetic and copies ran while one was open for 3% of the time, Pallas kernels for 0%

commit v1 on v0

--- a/solution.py
+++ b/solution.py
@@ -6,6 +6,34 @@
 BLK = 32
 TERMS = 6
 SQUARINGS = 2
+
+
+def _place_counts(local_x):
+    v_now, high, state_next = (lax.axis_size("row"), lax.axis_index("row"), local_x.shape[0])
+    r_now = lax.dynamic_update_slice_in_dim(
+        jnp.zeros(
+            [at * v_now if m == 0 else at for m, at in enumerate(local_x.shape)], local_x.dtype
+        ),
+        local_x,
+        high * state_next,
+        axis=0,
+    )
+    side_arr = local_next = local_x
+    for q in range(1, v_now // 2 + 1):
+        side_arr = lax.ppermute(
+            side_arr, "row", list(map(lambda m: (m, (m + 1) % v_now), range(v_now)))
+        )
+        r_now = lax.dynamic_update_slice_in_dim(
+            r_now, side_arr, (high - q) % v_now * state_next, axis=0
+        )
+        if 2 * q < v_now:
+            local_next = lax.ppermute(
+                local_next, "row", list(map(lambda m: (m, (m - 1) % v_now), range(v_now)))
+            )
+            r_now = lax.dynamic_update_slice_in_dim(
+                r_now, local_next, (high + q) % v_now * state_next, axis=0
+            )
+    return r_now
 
 
 def expand(mask, values):
@@ -22,11 +50,7 @@
 
 
 def panel_times(row_panel, matrix):
-    return jnp.dot(
-        row_panel,
-        lax.all_gather(matrix, "row", axis=0, tiled=True),
-        preferred_element_type=jnp.float32,
-    )
+    return jnp.dot(row_panel, _place_counts(matrix), preferred_element_type=jnp.float32)
 
 
 def reorder(generator, owner_order):

time: 757 us -> 824 us (1.089); the launches traced: 757 us -> 815 us
  waiting for transfers between devices: 683 us -> 271 us
  starting transfers between devices: 0.93 us -> 379 us
  local copies, waits for them, and re-layouts: 16.9 us -> 121 us
  matrix products: 38.5 us -> 25.1 us
    all_gather x10 -> x0, waiting for transfers between devices: 458 us -> none  [panel_times(): lax.all_gather(matrix, 'row', axis=0, tiled=True)]
    ppermute x0 -> x150, starting transfers between devices: none -> 379 us  [the longest x70 370 us: _place_counts(): lax.ppermute(local_next, 'row', list(map(lambda m: (m, (m - 1) % v_now),...]
    ppermute x0 -> x150, waiting for transfers between devices: none -> 205 us  [the longest x80 201 us: _place_counts(): lax.ppermute(side_arr, 'row', list(map(lambda m: (m, (m + 1) % v_now), ra...]
    all_gather x7, waiting for transfers between devices: 153 us -> 0.09 us  [panel_rows(): return lax.all_gather(matrix, 'col', axis=1, tiled=True)]
    dynamic_update_slice x0 -> x150, local copies, waits for them, and re-layouts: none -> 80.6 us  [the longest x80 42.5 us: _place_counts(): lax.dynamic_update_slice_in_dim(r_now, side_arr, (high - q) % v_now * sta...]
    dot_general x11, matrix products: 35.6 us -> 22.2 us  [panel_times(): jnp.dot(row_panel, _place_counts(matrix), preferred_element_type=jnp.floa...]
    mul x26, local copies, waits for them, and re-layouts: 10.8 us -> 21.2 us  [expand(): values.reshape(row_blocks, BLK, column_blocks, BLK)]
    unnamed x16 -> x52, local copies, waits for them, and re-layouts: 0.04 us -> 10.3 us
  transfers between devices with their start and end apart: 19 -> 159, of which waited for: 19 -> 78; matrix products, arithmetic and copies ran while one was open for 3% -> 14% of each run, Pallas kernels for 0% -> 0%
where the time goes in v1:
time: 824 us; the launch traced here: 815 us
  starting transfers between devices  379 us (46%)
  waiting for transfers between devices  271 us (33%)
  local copies, waits for them, and re-layouts  121 us (15%)
  matrix products  25.1 us (3%)
  between operations  15 us (2%)
    ppermute x70, starting transfers between devices, _place_counts(): lax.ppermute(local_next, 'row', list(map(lambda m: (m, (m - 1) % v_now),...  370 us
    ppermute x80, waiting for transfers between devices, _place_counts(): lax.ppermute(side_arr, 'row', list(map(lambda m: (m, (m + 1) % v_now), ra...  201 us
    all_gather x1, waiting for transfers between devices, reorder(): segment = lax.all_gather(generator, 'row', axis=0, tiled=True)  42.5 us
    dynamic_update_slice x80, local copies, waits for them, and re-layouts, _place_counts(): lax.dynamic_update_slice_in_dim(r_now, side_arr, (high - q) % v_now * sta...  42.5 us
    dynamic_update_slice x70, local copies, waits for them, and re-layouts, _place_counts(): lax.dynamic_update_slice_in_dim(r_now, local_next, (high + q) % v_now * s...  38.1 us
    all_gather x1, waiting for transfers between devices, reorder(): segment = lax.all_gather(by_rows, 'col', axis=1, tiled=True)  23.5 us
    dot_general x11, matrix products, panel_times(): jnp.dot(row_panel, _place_counts(matrix), preferred_element_type=jnp.floa...  22.2 us
    mul x26, local copies, waits for them, and re-layouts, expand(): values.reshape(row_blocks, BLK, column_blocks, BLK)  21.2 us
  transfers between devices with their start and end apart: 159, of which 78 were waited for; matrix products, arithmetic and copies ran while one was open for 14% of the time, Pallas kernels for 0%

profile of v1, /device:TPU:0, one launch (start us, length us, event | category | flops | bytes accessed | tf_op | source)
XLA Modules:
  0.0 815.2 jit_solution(6855958698867075641)
XLA Ops:
  69.6 5.6 collective-permute-start.13
  79.4 8.4 %collective-permute-done.14 = bf16[192,384]{1,0:T(8,128)(2,1)S(1)} collective-permute-done((bf16[192,384]{1,0:T(8,128)(2,1)S(1)}, bf16[192,384]{1,0:T(8,128)(2,1)S(1)}, u32[]{:S(2)}, u32[]{:S(2)}) %collective-permute-start.14) | collective-permute-done | bytes 147488 | tf_op jit(solution)/shard_map/ppermute | solution.py:23
  210.2 42.5 %all-gather.18.cloned.1.call-done = bf16[3072,384]{1,0:T(8,128)(2,1)} async-done(((bf16[192,384]{1,0:T(8,128)(2,1)}), bf16[3072,384]{1,0:T(8,128)(2,1)}) %all-gather.18.cloned.1.call-update) | async-done | bytes 2359312 | tf_op jit(solution)/shard_map/all_gather | solution.py:65
  257.5 23.5 %all-gather.20.cloned.1.call-done = bf16[192,3072]{0,1:T(8,128)(2,1)} async-done(((bf16[192,384]{0,1:T(8,128)(2,1)}), bf16[192,3072]{0,1:T(8,128)(2,1)}) %all-gather.20.cloned.1.call-update) | async-done | bytes 1179664 | tf_op jit(solution)/shard_map/all_gather | solution.py:72
  337.1 5.6 collective-permute-start.58
  347.5 7.1 collective-permute-done.59
  421.9 7.7 collective-permute-done.74
  468.9 5.6 collective-permute-start.84
  487.1 5.8 collective-permute-start.88
  497.3 7.6 collective-permute-done.89
  525.9 5.6 collective-permute-start.95
  535.8 5.7 collective-permute-start.97
  553.8 5.8 collective-permute-start.101
  563.5 5.8 collective-permute-start.103
  573.1 7.3 collective-permute-done.104
  602.6 5.6 collective-permute-start.110
  628.9 5.8 collective-permute-start.116
  638.9 5.8 collective-permute-start.118
  648.7 7.3 collective-permute-done.119
  696.1 5.7 collective-permute-start.129
  704.7 5.8 collective-permute-start.131
  714.5 5.8 collective-permute-start.133
  723.7 8.5 %collective-permute-done.134 = bf16[192,384]{1,0:T(8,128)(2,1)S(1)} collective-permute-done((bf16[192,384]{1,0:T(8,128)(2,1)S(1)}, bf16[192,384]{1,0:T(8,128)(2,1)S(1)}, u32[]{:S(2)}, u32[]{:S(2)}) %collective-permute-start.134) | collective-permute-done | bytes 147488 | tf_op jit(solution)/shard_map/ppermute | solution.py:23
  797.0 8.4 %collective-permute-done.149 = bf16[192,384]{1,0:T(8,128)(2,1)S(1)} collective-permute-done((bf16[192,384]{1,0:T(8,128)(2,1)S(1)}, bf16[192,384]{1,0:T(8,128)(2,1)S(1)}, u32[]{:S(2)}, u32[]{:S(2)}) %collective-permute-start.149) | collective-permute-done | bytes 147488 | tf_op jit(solution)/shard_map/ppermute | solution.py:23
  (575 shorter events, 592.0 us)
Async XLA Ops:
  6.5 81.3 %all-gather.14.cloned.1.call-start = ((), (), s32[]{:S(2)}) async-start(), calls=%async_computation.2 | async-start | bytes 1327104 | tf_op jit(solution)/shard_map/all_gather | solution.py:49
  10.3 143.3 %all-gather.10.cloned.1.call-start = ((), (), s32[]{:S(2)}) async-start(), calls=%async_computation | async-start | bytes 1327104 | tf_op jit(solution)/shard_map/all_gather | solution.py:49
  10.4 92.5 %collective-permute-start.15 = (bf16[192,384]{1,0:T(8,128)(2,1)}, bf16[192,384]{1,0:T(8,128)(2,1)S(1)}, u32[]{:S(2)}, u32[]{:S(2)}) collective-permute-start(bf16[192,384]{1,0:T(8,128)(2,1)} %get-tuple-element.8), channel_id=1, source_target_pairs={{0,8},{8,16},{16,24},{24,32},{32,40},{40,48},{48,56},{56,64},{64,7... | collective-permute-start | bytes 442376 | tf_op jit(solution)/shard_map/ppermute | solution.py:23
  22.5 181.2 %all-gather.16.cloned.1.call-start = ((), (), s32[]{:S(2)}) async-start(), calls=%async_computation.3 | async-start | bytes 1327104 | tf_op jit(solution)/shard_map/all_gather | solution.py:49
  90.6 115.9 %all-gather.12.cloned.1.call-start = ((), (), s32[]{:S(2)}) async-start(), calls=%async_computation.1 | async-start | bytes 1327104 | tf_op jit(solution)/shard_map/all_gather | solution.py:49
  90.8 19.9 %collective-permute-start.30 = (bf16[192,384]{1,0:T(8,128)(2,1)S(1)}, bf16[192,384]{1,0:T(8,128)(2,1)}, u32[]{:S(2)}, u32[]{:S(2)}) collective-permute-start(bf16[192,384]{1,0:T(8,128)(2,1)S(1)} %copy-done.14), channel_id=1, source_target_pairs={{0,8},{8,16},{16,24},{24,32},{32,40},{40,48},{48,56},{56,64},{64,7... | collective-permute-start | bytes 442376 | tf_op jit(solution)/shard_map/ppermute | solution.py:23
  92.8 19.5 %collective-permute-start.31 = (bf16[192,384]{1,0:T(8,128)(2,1)S(1)}, bf16[192,384]{1,0:T(8,128)(2,1)}, u32[]{:S(2)}, u32[]{:S(2)}) collective-permute-start(bf16[192,384]{1,0:T(8,128)(2,1)S(1)} %copy-done.14), channel_id=1, source_target_pairs={{0,120},{8,0},{16,8},{24,16},{32,24},{40,32},{48,40},{56,48},{64,5... | collective-permute-start | bytes 442376 | tf_op jit(solution)/shard_map/ppermute | solution.py:30
  102.9 16.3 %collective-permute-start.17 = (bf16[192,384]{1,0:T(8,128)(2,1)S(1)}, bf16[192,384]{1,0:T(8,128)(2,1)S(1)}, u32[]{:S(2)}, u32[]{:S(2)}) collective-permute-start(bf16[192,384]{1,0:T(8,128)(2,1)S(1)} %collective-permute-done.15), channel_id=1, source_target_pairs={{0,8},{8,16},{16,24},{24,32},{32,40},{40,48},{48,56},{56,64},{64,7... | collective-permute-start | bytes 442376 | tf_op jit(solution)/shard_map/ppermute | solution.py:23
  103.7 16.2 %collective-permute-start.18 = (bf16[192,384]{1,0:T(8,128)(2,1)}, bf16[192,384]{1,0:T(8,128)(2,1)S(1)}, u32[]{:S(2)}, u32[]{:S(2)}) collective-permute-start(bf16[192,384]{1,0:T(8,128)(2,1)} %collective-permute-done.16), channel_id=1, source_target_pairs={{0,120},{8,0},{16,8},{24,16},{32,24},{40,32},{48,40},{56,48},{64,5... | collective-permute-start | bytes 442376 | tf_op jit(solution)/shard_map/ppermute | solution.py:30
  110.7 15.3 %collective-permute-start.32 = (bf16[192,384]{1,0:T(8,128)(2,1)}, bf16[192,384]{1,0:T(8,128)(2,1)S(1)}, u32[]{:S(2)}, u32[]{:S(2)}) collective-permute-start(bf16[192,384]{1,0:T(8,128)(2,1)} %collective-permute-done.30), channel_id=1, source_target_pairs={{0,8},{8,16},{16,24},{24,32},{32,40},{40,48},{48,56},{56,64},{64,7... | collective-permute-start | bytes 442376 | tf_op jit(solution)/shard_map/ppermute | solution.py:23
  112.3 14.3 %collective-permute-start.33 = (bf16[192,384]{1,0:T(8,128)(2,1)}, bf16[192,384]{1,0:T(8,128)(2,1)S(1)}, u32[]{:S(2)}, u32[]{:S(2)}) collective-permute-start(bf16[192,384]{1,0:T(8,128)(2,1)} %collective-permute-done.31), channel_id=1, source_target_pairs={{0,120},{8,0},{16,8},{24,16},{32,24},{40,32},{48,40},{56,48},{64,5... | collective-permute-start | bytes 442376 | tf_op jit(solution)/shard_map/ppermute | solution.py:30
  126.6 13.4 %collective-permute-start.35 = (bf16[192,384]{1,0:T(8,128)(2,1)S(1)}, bf16[192,384]{1,0:T(8,128)(2,1)S(1)}, u32[]{:S(2)}, u32[]{:S(2)}) collective-permute-start(bf16[192,384]{1,0:T(8,128)(2,1)S(1)} %collective-permute-done.33), channel_id=1, source_target_pairs={{0,120},{8,0},{16,8},{24,16},{32,24},{40,32},{48,40},{56,48},{64,5... | collective-permute-start | bytes 442376 | tf_op jit(solution)/shard_map/ppermute | solution.py:30
  140.1 18.0 %collective-permute-start.37 = (bf16[192,384]{1,0:T(8,128)(2,1)S(1)}, bf16[192,384]{1,0:T(8,128)(2,1)}, u32[]{:S(2)}, u32[]{:S(2)}) collective-permute-start(bf16[192,384]{1,0:T(8,128)(2,1)S(1)} %collective-permute-done.35), channel_id=1, source_target_pairs={{0,120},{8,0},{16,8},{24,16},{32,24},{40,32},{48,40},{56,48},{64,5... | collective-permute-start | bytes 442376 | tf_op jit(solution)/shard_map/ppermute | solution.py:30
  146.1 19.0 %collective-permute-start.23 = (bf16[192,384]{1,0:T(8,128)(2,1)S(1)}, bf16[192,384]{1,0:T(8,128)(2,1)}, u32[]{:S(2)}, u32[]{:S(2)}) collective-permute-start(bf16[192,384]{1,0:T(8,128)(2,1)S(1)} %collective-permute-done.21), channel_id=1, source_target_pairs={{0,8},{8,16},{16,24},{24,32},{32,40},{40,48},{48,56},{56,64},{64,7... | collective-permute-start | bytes 442376 | tf_op jit(solution)/shard_map/ppermute | solution.py:23
  146.1 20.6 %collective-permute-start.24 = (bf16[192,384]{1,0:T(8,128)(2,1)}, bf16[192,384]{1,0:T(8,128)(2,1)S(1)}, u32[]{:S(2)}, u32[]{:S(2)}) collective-permute-start(bf16[192,384]{1,0:T(8,128)(2,1)} %collective-permute-done.22), channel_id=1, source_target_pairs={{0,120},{8,0},{16,8},{24,16},{32,24},{40,32},{48,40},{56,48},{64,5... | collective-permute-start | bytes 442376 | tf_op jit(solution)/shard_map/ppermute | solution.py:30
  151.4 21.2 %collective-permute-start.38 = (bf16[192,384]{1,0:T(8,128)(2,1)}, bf16[192,384]{1,0:T(8,128)(2,1)S(1)}, u32[]{:S(2)}, u32[]{:S(2)}) collective-permute-start(bf16[192,384]{1,0:T(8,128)(2,1)} %collective-permute-done.36), channel_id=1, source_target_pairs={{0,8},{8,16},{16,24},{24,32},{32,40},{40,48},{48,56},{56,64},{64,7... | collective-permute-start | bytes 442376 | tf_op jit(solution)/shard_map/ppermute | solution.py:23
  156.4 96.3 %all-gather.18.cloned.1.call-start = ((), (), s32[]{:S(2)}) async-start(), calls=%async_computation.4 | async-start | bytes 2506752 | tf_op jit(solution)/shard_map/all_gather | solution.py:65
  158.0 15.3 %collective-permute-start.39 = (bf16[192,384]{1,0:T(8,128)(2,1)}, bf16[192,384]{1,0:T(8,128)(2,1)S(1)}, u32[]{:S(2)}, u32[]{:S(2)}) collective-permute-start(bf16[192,384]{1,0:T(8,128)(2,1)} %collective-permute-done.37), channel_id=1, source_target_pairs={{0,120},{8,0},{16,8},{24,16},{32,24},{40,32},{48,40},{56,48},{64,5... | collective-permute-start | bytes 442376 | tf_op jit(solution)/shard_map/ppermute | solution.py:30
  165.0 14.3 %collective-permute-start.25 = (bf16[192,384]{1,0:T(8,128)(2,1)}, bf16[192,384]{1,0:T(8,128)(2,1)S(1)}, u32[]{:S(2)}, u32[]{:S(2)}) collective-permute-start(bf16[192,384]{1,0:T(8,128)(2,1)} %collective-permute-done.23), channel_id=1, source_target_pairs={{0,8},{8,16},{16,24},{24,32},{32,40},{40,48},{48,56},{56,64},{64,7... | collective-permute-start | bytes 442376 | tf_op jit(solution)/shard_map/ppermute | solution.py:23
  180.0 15.2 %collective-permute-start.28 = (bf16[192,384]{1,0:T(8,128)(2,1)S(1)}, bf16[192,384]{1,0:T(8,128)(2,1)S(1)}, u32[]{:S(2)}, u32[]{:S(2)}) collective-permute-start(bf16[192,384]{1,0:T(8,128)(2,1)S(1)} %collective-permute-done.26), channel_id=1, source_target_pairs={{0,120},{8,0},{16,8},{24,16},{32,24},{40,32},{48,40},{56,48},{64,5... | collective-permute-start | bytes 442376 | tf_op jit(solution)/shard_map/ppermute | solution.py:30
  210.0 70.9 %all-gather.20.cloned.1.call-start = ((), (), s32[]{:S(2)}) async-start(), calls=%async_computation.5 | async-start | bytes 1769472 | tf_op jit(solution)/shard_map/all_gather | solution.py:72
  257.3 97.9 %all-gather.22.cloned.1.call-start = ((), (), s32[]{:S(2)}) async-start(), calls=%async_computation.6 | async-start | bytes 1769472 | tf_op jit(solution)/shard_map/all_gather | solution.py:49
  284.1 448.2 %all-gather.24.cloned.1.call-start = ((), (), s32[]{:S(2)}) async-start(), calls=%async_computation.7 | async-start | bytes 1327104 | tf_op jit(solution)/shard_map/all_gather | solution.py:49
  659.9 145.6 %all-gather.26.cloned.1.call-start = ((), (), s32[]{:S(2)}) async-start(), calls=%async_computation.8 | async-start | bytes 1327104 | tf_op jit(solution)/shard_map/all_gather | solution.py:49
  (161 other events, 1472.3 us)
Sparse Core Ops, SparseCore 0:
  10.5 25.9 all-gather.13
  38.2 23.4 all-gather.9
  90.7 19.7 all-gather.15
  156.5 24.5 all-gather.11
  210.2 42.4 all-gather.17
  257.4 23.4 all-gather.19
  284.2 24.4 all-gather.21
  660.0 18.7 all-gather.23
  736.6 18.7 all-gather.25
